TPU v7x, 32 devices: a whole 2x2x4 slice. The times are simulated.
32 devices in a mesh: row: 4 (over y, x), col: 8 (over z, core).
Axes of the slice: x: 2, y: 2, z: 4, core: 2. Of those that a mesh axis runs over, the one named last changes fastest.
Arguments:
- transmission: float32 [2, 2, 512, 1024], P(None, None, 'row', 'col'), may hold values from -6 to 6
- probe: float32 [2, 256, 256], replicated, may hold values from -6 to 6
- fresnel_phase: float32 [256, 256], replicated, may hold values from -3.140625 to 3.140625
- amplitudes: float32 [4, 8, 1, 256, 256], P('row', 'col'), may hold values from 0.3 to 4
- positions: int32 [4, 8, 1, 2], P('row', 'col'), may hold values from 0 to 72, as said below
- tv_weight: float32 [512, 1024], P('row', 'col'), may hold values from 0.3 to 3
Outputs:
- refined: float32 [2, 2, 512, 1024], P(None, None, 'row', 'col')
Inputs may be any that keep to these rules, and one draw needn't show every extreme that they name: `positions`: over all tiles and views together, for each of the two coordinates, some view has offset 0 and some view has offset 2 * 36; a view covers rows and columns [offset, offset + 256) of its tile's region.
All inputs are finite; a program needn't handle non-finite values.
Results may differ from a plain program's by a relative error of at most 0.00016.
Values sent between devices are 32-bit elements; how exact they have to be, the bound alone decides.
A program may use at most 64 MiB of HBM per device.

v0:
```python
import math

import jax
import jax.numpy as jnp
from jax import lax
from jax.sharding import PartitionSpec as P

CORE = 128
PROBE = 256
VIEWS = 1
SLICES = 2
TV_STEPS = 3
HALO = 100
EXTENT = 328


AMP_EPS = 0.1
LEARN_RATE = 0.2
TV_EPS = 1.0
TV_TAU = 0.1
HIGHEST = lax.Precision.HIGHEST


def passed_along(value, axis, steps):
    count = lax.axis_size(axis)
    first, last = (max(0, -steps), min(count, count - steps))
    return lax.ppermute(value, axis, [(source, source + steps) for source in range(first, last)])


def padded(value, sides, width):
    for axis, dim in sides:
        peers, length = (lax.axis_size(axis), value.shape[dim])
        up = [(i, (i + 1) % peers) for i in range(peers - 1)]
        down = [(j, i) for i, j in up]
        last = lax.slice_in_dim(value, length - width, length, axis=dim)
        first = lax.slice_in_dim(value, 0, width, axis=dim)
        before = lax.ppermute(last, axis, up)
        after = lax.ppermute(first, axis, down)
        value = jnp.concatenate([before, value, after], axis=dim)
    return value


def dft_table(length, sign):
    index = jnp.arange(length, dtype=jnp.int32)
    phase = index[:, None] * index[None, :] % length
    angle = phase.astype(jnp.float32) * (2.0 * math.pi / length)
    factor = 1.0 / math.sqrt(length)
    return (jnp.cos(angle) * factor, sign * factor * jnp.sin(angle))


def transform(real_in, imag_in, table):
    cosine, sine = table
    length = real_in.shape[0]
    product = jnp.dot(
        jnp.concatenate([cosine, sine], axis=0),
        jnp.concatenate([real_in, imag_in], axis=1),
        precision=HIGHEST,
    )
    left_real = product[:length, :length] - product[length:, length:]
    left_imag = product[:length, length:] + product[length:, :length]
    product = jnp.dot(
        jnp.concatenate([left_real, left_imag], axis=0),
        jnp.concatenate([cosine, sine], axis=1),
        precision=HIGHEST,
    )
    return (
        product[:length, :length] - product[length:, length:],
        product[:length, length:] + product[length:, :length],
    )


def view_gradient(extended, probe, kernel, measured, offset, forward, inverse):
    anchor = jnp.zeros((), jnp.int32)
    windows = [
        lax.dynamic_slice(extended[s], (anchor, offset[0], offset[1]), (2, PROBE, PROBE))
        for s in range(SLICES)
    ]
    wave_real, wave_imag = (probe[0], probe[1])
    kernel_real, kernel_imag = kernel
    incoming = []
    for s in range(SLICES):
        incoming.append((wave_real, wave_imag))
        exit_real = windows[s][0] * wave_real - windows[s][1] * wave_imag
        exit_imag = windows[s][0] * wave_imag + windows[s][1] * wave_real
        if s < SLICES - 1:
            freq_real, freq_imag = transform(exit_real, exit_imag, forward)
            wave_real, wave_imag = transform(
                kernel_real * freq_real - kernel_imag * freq_imag,
                kernel_real * freq_imag + kernel_imag * freq_real,
                inverse,
            )
    far_real, far_imag = transform(exit_real, exit_imag, forward)
    magnitude = jnp.sqrt(far_real * far_real + far_imag * far_imag + AMP_EPS)
    factor = 1.0 - measured / magnitude
    back_real, back_imag = transform(far_real * factor, far_imag * factor, inverse)
    gradients = []
    for s in range(SLICES - 1, -1, -1):
        in_real, in_imag = incoming[s]
        gradients.insert(
            0,
            jnp.stack(
                [
                    in_real * back_real + in_imag * back_imag,
                    in_real * back_imag - in_imag * back_real,
                ]
            ),
        )
        if s > 0:
            pulled_real = windows[s][0] * back_real + windows[s][1] * back_imag
            pulled_imag = windows[s][0] * back_imag - windows[s][1] * back_real
            freq_real, freq_imag = transform(pulled_real, pulled_imag, forward)
            back_real, back_imag = transform(
                kernel_real * freq_real + kernel_imag * freq_imag,
                kernel_real * freq_imag - kernel_imag * freq_real,
                inverse,
            )
    return jnp.stack(gradients)


def fold_rows(summed):
    kept = summed[:, :, HALO : HALO + CORE, :]
    for by in (1, -1):
        border = summed[:, :, HALO + CORE :, :] if by == 1 else summed[:, :, :HALO, :]
        arrived = passed_along(border, "row", by)
        if by == 1:
            kept = kept.at[:, :, :HALO, :].add(arrived)
        else:
            kept = kept.at[:, :, CORE - HALO :, :].add(arrived)
    return kept


def fold_cols(summed):
    kept = summed[:, :, :, HALO : HALO + CORE]
    for by in (1, -1):
        border = summed[:, :, :, HALO + CORE :] if by == 1 else summed[:, :, :, :HALO]
        arrived = passed_along(border, "col", by)
        if by == 1:
            kept = kept.at[:, :, :, :HALO].add(arrived)
        else:
            kept = kept.at[:, :, :, CORE - HALO :].add(arrived)
    return kept


def inside_mask(width):
    span_steps = jnp.arange(CORE + 2 * width, dtype=jnp.int32) - width
    row_global = lax.axis_index("row") * CORE + span_steps
    col_global = lax.axis_index("col") * CORE + span_steps
    row_inside = (row_global >= 0) & (row_global < lax.axis_size("row") * CORE)
    col_inside = (col_global >= 0) & (col_global < lax.axis_size("col") * CORE)
    return (row_inside[:, None] & col_inside[None, :]).astype(jnp.float32)


def tv_update(field, weight, inside):
    down_diff = field[:, :, 1:, :-1] - field[:, :, :-1, :-1]
    right_diff = field[:, :, :-1, 1:] - field[:, :, :-1, :-1]
    spread = jnp.sqrt(
        jnp.sum(down_diff * down_diff + right_diff * right_diff, axis=1, keepdims=True) + TV_EPS
    )
    gating = weight[:-1, :-1] * inside[:-1, :-1]
    down_flux = gating * down_diff / spread
    right_flux = gating * right_diff / spread
    update = (
        down_flux[:, :, 1:, 1:]
        - down_flux[:, :, :-1, 1:]
        + right_flux[:, :, 1:, 1:]
        - right_flux[:, :, 1:, :-1]
    )
    return (field[:, :, 1:-1, 1:-1] + TV_TAU * update) * inside[1:-1, 1:-1]


def body(transmission, probe, fresnel_phase, amplitudes, positions, tv_weight):
    forward = dft_table(PROBE, -1.0)
    inverse = dft_table(PROBE, 1.0)
    kernel = (jnp.cos(fresnel_phase), jnp.sin(fresnel_phase))
    extended = padded(transmission, (("row", 2), ("col", 3)), HALO)
    anchor = jnp.zeros((), jnp.int32)

    def add_view(v, summed):
        offset = positions[0, 0, v]
        gradient = view_gradient(
            extended, probe, kernel, amplitudes[0, 0, v], offset, forward, inverse
        )
        place = (anchor, anchor, offset[0], offset[1])
        current = lax.dynamic_slice(summed, place, (SLICES, 2, PROBE, PROBE))
        return lax.dynamic_update_slice(summed, current + gradient, place)

    summed = lax.fori_loop(0, VIEWS, add_view, jnp.zeros((SLICES, 2, EXTENT, EXTENT), jnp.float32))
    gradient = fold_cols(fold_rows(summed))
    field = transmission - LEARN_RATE * gradient
    channels = 2 * SLICES
    stacked = jnp.concatenate([field.reshape(channels, CORE, CORE), tv_weight[None]], axis=0)
    grown = padded(stacked, (("row", 1), ("col", 2)), TV_STEPS)
    weight_ext = grown[channels]
    field_ext = grown[:channels].reshape(SLICES, 2, CORE + 2 * TV_STEPS, CORE + 2 * TV_STEPS)
    inside = inside_mask(TV_STEPS)
    for step in range(TV_STEPS):
        field_ext = tv_update(field_ext, weight_ext, inside)
        weight_ext = weight_ext[1:-1, 1:-1]
        inside = inside[1:-1, 1:-1]
    field = field_ext
    return field


def solution(mesh):
    placed = (
        P(None, None, "row", "col"),
        P(),
        P(),
        P("row", "col", None, None, None),
        P("row", "col", None, None),
        P("row", "col"),
    )
    return jax.shard_map(
        body, mesh=mesh, in_specs=placed, out_specs=P(None, None, "row", "col"), check_vma=False
    )
```

profile of v0, /device:TPU:9, one launch (start us, length us, event | category | flops | bytes accessed | tf_op | source)
XLA Modules:
  0.0 138.3 jit_solution(13181150530919531773)
XLA Ops:
  1.1 3.1 %collective-permute-start = (f32[2,2,100,128]{3,2,1,0:T(8,128)S(1)}, f32[2,2,100,128]{3,2,1,0:T(8,128)S(1)}, u32[]{:S(2)}, u32[]{:S(2)}) collective-permute-start(f32[2,2,100,128]{3,2,1,0:T(8,128)S(1)} %get-tuple-element.193), channel_id=1, source_target_pairs={{0,8},{8,16},{16,24},{1,9},{9,17},{17,25},{2,10},{10,18},{18,26},{... | collective-permute-start | bytes 614408 | tf_op jit(solution)/shard_map/ppermute | solution.py:37
  4.2 1.3 collective-permute-start.1
  5.5 2.6 %collective-permute-done = f32[2,2,100,128]{3,2,1,0:T(8,128)S(1)} collective-permute-done((f32[2,2,100,128]{3,2,1,0:T(8,128)S(1)}, f32[2,2,100,128]{3,2,1,0:T(8,128)S(1)}, u32[]{:S(2)}, u32[]{:S(2)}) %collective-permute-start) | collective-permute-done | bytes 204832 | tf_op jit(solution)/shard_map/ppermute | solution.py:37
  8.1 6.5 %collective-permute-done.1 = f32[2,2,100,128]{3,2,1,0:T(8,128)S(1)} collective-permute-done((f32[2,2,100,128]{3,2,1,0:T(8,128)S(1)}, f32[2,2,100,128]{3,2,1,0:T(8,128)S(1)}, u32[]{:S(2)}, u32[]{:S(2)}) %collective-permute-start.1) | collective-permute-done | bytes 204832 | tf_op jit(solution)/shard_map/ppermute | solution.py:38
  16.2 4.6 %collective-permute-start.2 = (f32[2,2,328,100]{2,1,3,0:T(2,128)S(1)}, f32[2,2,328,100]{2,1,3,0:T(2,128)}, u32[]{:S(2)}, u32[]{:S(2)}) collective-permute-start(f32[2,2,328,100]{2,1,3,0:T(2,128)S(1)} %copy.11), channel_id=1, source_target_pairs={{0,1},{1,2},{2,3},{3,4},{4,5},{5,6},{6,7},{8,9},{9,10},{10,11},{11... | collective-permute-start | bytes 1574408 | tf_op jit(solution)/shard_map/ppermute | solution.py:37
  22.0 1.9 %collective-permute-start.3 = (f32[2,2,328,100]{2,1,3,0:T(2,128)}, f32[2,2,328,100]{2,1,3,0:T(2,128)}, u32[]{:S(2)}, u32[]{:S(2)}) collective-permute-start(f32[2,2,328,100]{2,1,3,0:T(2,128)} %copy.12), channel_id=1, source_target_pairs={{1,0},{2,1},{3,2},{4,3},{5,4},{6,5},{7,6},{9,8},{10,9},{11,10},{12... | collective-permute-start | bytes 1574408 | tf_op jit(solution)/shard_map/ppermute | solution.py:38
  30.9 1.3 copy.13
  32.2 1.5 %collective-permute-done.3 = f32[2,2,328,100]{2,1,3,0:T(2,128)} collective-permute-done((f32[2,2,328,100]{2,1,3,0:T(2,128)}, f32[2,2,328,100]{2,1,3,0:T(2,128)}, u32[]{:S(2)}, u32[]{:S(2)}) %collective-permute-start.3) | collective-permute-done | bytes 524832 | tf_op jit(solution)/shard_map/ppermute | solution.py:38
  33.7 1.3 copy.14
  53.9 14.3 %dynamic_update_slice.6 = f32[2,2,328,328]{3,2,1,0:T(8,128)S(1)} dynamic-update-slice(f32[2,2,328,328]{3,2,1,0:T(8,128)S(1)} %broadcast_in_dim.4, f32[2,2,256,256]{3,2,1,0:T(8,128)} %pad_maximum_fusion.1, s32[]{:T(128)} %constant.172.clone.1, s32[]{:T(128)} %constant.172.clone.1, s32[]{:T(128)S(6)} %select_n.45, s32[]{:T(128)S(6)} %select_n.46) | dynamic-update-slice | bytes 2097156 | tf_op jit(solution)/shard_map/while/body/eval_jaxpr/dynamic_update_slice | solution.py:185
  69.2 2.6 %collective-permute-start.4 = (f32[2,2,100,328]{3,2,1,0:T(8,128)S(1)}, f32[2,2,100,328]{3,2,1,0:T(8,128)S(1)}, u32[]{:S(2)}, u32[]{:S(2)}) collective-permute-start(f32[2,2,100,328]{3,2,1,0:T(8,128)S(1)} %get-tuple-element.149), channel_id=1, source_target_pairs={{0,8},{8,16},{16,24},{1,9},{9,17},{17,25},{2,10},{10,18},{18,26},{... | collective-permute-start | bytes 1574408 | tf_op jit(solution)/shard_map/ppermute | solution.py:27
  71.8 1.3 collective-permute-start.5
  73.2 12.0 %collective-permute-done.4 = f32[2,2,100,328]{3,2,1,0:T(8,128)S(1)} collective-permute-done((f32[2,2,100,328]{3,2,1,0:T(8,128)S(1)}, f32[2,2,100,328]{3,2,1,0:T(8,128)S(1)}, u32[]{:S(2)}, u32[]{:S(2)}) %collective-permute-start.4) | collective-permute-done | bytes 524832 | tf_op jit(solution)/shard_map/ppermute | solution.py:27
  86.0 3.3 %scatter-add.14 = f32[2,2,128,328]{3,2,1,0:T(8,128)S(1)} dynamic-update-slice(f32[2,2,128,328]{3,2,1,0:T(8,128)S(1)} %slice.808, f32[2,2,100,328]{3,2,1,0:T(8,128)} %slice_add_fusion.1, s32[]{:T(128)} %constant.172.clone.1, s32[]{:T(128)} %constant.172.clone.1, s32[]{:T(128)} %constant.172.clone.1, s32[]{:T(128)} %constant.172.clone.1) | dynamic-update-slice | bytes 1049604 | tf_op jit(solution)/shard_map/scatter-add | solution.py:126
  89.3 9.8 %collective-permute-done.5 = f32[2,2,100,328]{3,2,1,0:T(8,128)} collective-permute-done((f32[2,2,100,328]{3,2,1,0:T(8,128)}, f32[2,2,100,328]{3,2,1,0:T(8,128)}, u32[]{:S(2)}, u32[]{:S(2)}) %collective-permute-start.5) | collective-permute-done | bytes 524832 | tf_op jit(solution)/shard_map/ppermute | solution.py:27
  100.2 1.6 %scatter-add.15 = f32[2,2,128,328]{3,2,1,0:T(8,128)S(1)} dynamic-update-slice(f32[2,2,128,328]{3,2,1,0:T(8,128)S(1)} %scatter-add.14, f32[2,2,100,328]{3,2,1,0:T(8,128)S(1)} %slice_add_fusion, s32[]{:T(128)} %constant.172.clone.1, s32[]{:T(128)} %constant.172.clone.1, s32[]{:T(128)} %constant.181.clone.1, s32[]{:T(128)} %constant.172.clone.1) | dynamic-update-slice | bytes 1049604 | tf_op jit(solution)/shard_map/scatter-add | solution.py:128
  102.0 4.4 %collective-permute-start.6 = (f32[2,2,128,100]{3,2,1,0:T(8,128)S(1)}, f32[2,2,128,100]{3,2,1,0:T(8,128)S(1)}, u32[]{:S(2)}, u32[]{:S(2)}) collective-permute-start(f32[2,2,128,100]{3,2,1,0:T(8,128)S(1)} %get-tuple-element.183), channel_id=1, source_target_pairs={{0,1},{1,2},{2,3},{3,4},{4,5},{5,6},{6,7},{8,9},{9,10},{10,11},{11... | collective-permute-start | bytes 614408 | tf_op jit(solution)/shard_map/ppermute | solution.py:27
  106.5 1.9 %collective-permute-start.7 = (f32[2,2,128,100]{3,2,1,0:T(8,128)S(1)}, f32[2,2,128,100]{3,2,1,0:T(8,128)S(1)}, u32[]{:S(2)}, u32[]{:S(2)}) collective-permute-start(f32[2,2,128,100]{3,2,1,0:T(8,128)S(1)} %get-tuple-element.182), channel_id=1, source_target_pairs={{1,0},{2,1},{3,2},{4,3},{5,4},{6,5},{7,6},{9,8},{10,9},{11,10},{12... | collective-permute-start | bytes 614408 | tf_op jit(solution)/shard_map/ppermute | solution.py:27
  110.3 3.9 %collective-permute-done.7 = f32[2,2,128,100]{3,2,1,0:T(8,128)S(1)} collective-permute-done((f32[2,2,128,100]{3,2,1,0:T(8,128)S(1)}, f32[2,2,128,100]{3,2,1,0:T(8,128)S(1)}, u32[]{:S(2)}, u32[]{:S(2)}) %collective-permute-start.7) | collective-permute-done | bytes 204832 | tf_op jit(solution)/shard_map/ppermute | solution.py:27
  118.3 3.1 %collective-permute-done.9 = f32[5,3,128]{2,1,0:T(4,128)S(1)} collective-permute-done((f32[5,3,128]{2,1,0:T(4,128)S(1)}, f32[5,3,128]{2,1,0:T(4,128)S(1)}, u32[]{:S(2)}, u32[]{:S(2)}) %collective-permute-start.9) | collective-permute-done | bytes 7712 | tf_op jit(solution)/shard_map/ppermute | solution.py:38
  121.6 3.1 %collective-permute-start.10 = (f32[5,134,3]{2,1,0:T(8,128)S(1)}, f32[5,134,3]{2,1,0:T(8,128)S(1)}, u32[]{:S(2)}, u32[]{:S(2)}) collective-permute-start(f32[5,134,3]{2,1,0:T(8,128)S(1)} %get-tuple-element.187), channel_id=1, source_target_pairs={{0,1},{1,2},{2,3},{3,4},{4,5},{5,6},{6,7},{8,9},{9,10},{10,11},{11... | collective-permute-start | bytes 24128 | tf_op jit(solution)/shard_map/ppermute | solution.py:37
  124.7 2.2 %collective-permute-start.11 = (f32[5,134,3]{2,1,0:T(8,128)S(1)}, f32[5,134,3]{2,1,0:T(8,128)S(1)}, u32[]{:S(2)}, u32[]{:S(2)}) collective-permute-start(f32[5,134,3]{2,1,0:T(8,128)S(1)} %get-tuple-element.188), channel_id=1, source_target_pairs={{1,0},{2,1},{3,2},{4,3},{5,4},{6,5},{7,6},{9,8},{10,9},{11,10},{12... | collective-permute-start | bytes 24128 | tf_op jit(solution)/shard_map/ppermute | solution.py:38
  127.3 1.6 %collective-permute-done.10 = f32[5,134,3]{2,1,0:T(8,128)S(1)} collective-permute-done((f32[5,134,3]{2,1,0:T(8,128)S(1)}, f32[5,134,3]{2,1,0:T(8,128)S(1)}, u32[]{:S(2)}, u32[]{:S(2)}) %collective-permute-start.10) | collective-permute-done | bytes 8072 | tf_op jit(solution)/shard_map/ppermute | solution.py:37
  128.9 4.4 %collective-permute-done.11 = f32[5,134,3]{2,1,0:T(8,128)S(1)} collective-permute-done((f32[5,134,3]{2,1,0:T(8,128)S(1)}, f32[5,134,3]{2,1,0:T(8,128)S(1)}, u32[]{:S(2)}, u32[]{:S(2)}) %collective-permute-start.11) | collective-permute-done | bytes 8072 | tf_op jit(solution)/shard_map/ppermute | solution.py:38
  (97 shorter events, 40.0 us)
Async XLA Ops:
  1.1 7.0 %collective-permute-start = (f32[2,2,100,128]{3,2,1,0:T(8,128)S(1)}, f32[2,2,100,128]{3,2,1,0:T(8,128)S(1)}, u32[]{:S(2)}, u32[]{:S(2)}) collective-permute-start(f32[2,2,100,128]{3,2,1,0:T(8,128)S(1)} %get-tuple-element.193), channel_id=1, source_target_pairs={{0,8},{8,16},{16,24},{1,9},{9,17},{17,25},{2,10},{10,18},{18,26},{... | collective-permute-start | bytes 614408 | tf_op jit(solution)/shard_map/ppermute | solution.py:37
  4.2 10.4 %collective-permute-start.1 = (f32[2,2,100,128]{3,2,1,0:T(8,128)S(1)}, f32[2,2,100,128]{3,2,1,0:T(8,128)S(1)}, u32[]{:S(2)}, u32[]{:S(2)}) collective-permute-start(f32[2,2,100,128]{3,2,1,0:T(8,128)S(1)} %get-tuple-element.194), channel_id=1, source_target_pairs={{8,0},{16,8},{24,16},{9,1},{17,9},{25,17},{10,2},{18,10},{26,18},{... | collective-permute-start | bytes 614408 | tf_op jit(solution)/shard_map/ppermute | solution.py:38
  15.6 8.3 %copy-start.5 = (s32[1,1,1,2]{3,2,1,0:T(1,128)S(1)}, s32[1,1,1,2]{3,2,1,0:T(1,128)}, u32[]{:S(2)}) copy-start(s32[1,1,1,2]{3,2,1,0:T(1,128)} %param.18) | copy-start | bytes 28
  15.6 11.4 %copy-start.3 = (f32[256,256]{1,0:T(8,128)S(1)}, f32[256,256]{1,0:T(8,128)}, u32[]{:S(2)}) copy-start(f32[256,256]{1,0:T(8,128)} %param.16) | copy-start | bytes 786436
  15.9 11.3 %copy-start.4 = (f32[1,1,1,256,256]{4,3,2,1,0:T(8,128)S(1)}, f32[1,1,1,256,256]{4,3,2,1,0:T(8,128)}, u32[]{:S(2)}) copy-start(f32[1,1,1,256,256]{4,3,2,1,0:T(8,128)} %param.17) | copy-start | bytes 786436
  16.2 14.6 %collective-permute-start.2 = (f32[2,2,328,100]{2,1,3,0:T(2,128)S(1)}, f32[2,2,328,100]{2,1,3,0:T(2,128)}, u32[]{:S(2)}, u32[]{:S(2)}) collective-permute-start(f32[2,2,328,100]{2,1,3,0:T(2,128)S(1)} %copy.11), channel_id=1, source_target_pairs={{0,1},{1,2},{2,3},{3,4},{4,5},{5,6},{6,7},{8,9},{9,10},{10,11},{11... | collective-permute-start | bytes 1574408 | tf_op jit(solution)/shard_map/ppermute | solution.py:37
  22.0 11.8 %collective-permute-start.3 = (f32[2,2,328,100]{2,1,3,0:T(2,128)}, f32[2,2,328,100]{2,1,3,0:T(2,128)}, u32[]{:S(2)}, u32[]{:S(2)}) collective-permute-start(f32[2,2,328,100]{2,1,3,0:T(2,128)} %copy.12), channel_id=1, source_target_pairs={{1,0},{2,1},{3,2},{4,3},{5,4},{6,5},{7,6},{9,8},{10,9},{11,10},{12... | collective-permute-start | bytes 1574408 | tf_op jit(solution)/shard_map/ppermute | solution.py:38
  27.3 7.8 %copy-start = (f32[2,2,128,128]{3,2,1,0:T(8,128)S(1)}, f32[2,2,128,128]{3,2,1,0:T(8,128)}, u32[]{:S(2)}) copy-start(f32[2,2,128,128]{3,2,1,0:T(8,128)} %param.14) | copy-start | bytes 786436
  35.9 1.0 copy-start.1
  69.2 15.9 %collective-permute-start.4 = (f32[2,2,100,328]{3,2,1,0:T(8,128)S(1)}, f32[2,2,100,328]{3,2,1,0:T(8,128)S(1)}, u32[]{:S(2)}, u32[]{:S(2)}) collective-permute-start(f32[2,2,100,328]{3,2,1,0:T(8,128)S(1)} %get-tuple-element.149), channel_id=1, source_target_pairs={{0,8},{8,16},{16,24},{1,9},{9,17},{17,25},{2,10},{10,18},{18,26},{... | collective-permute-start | bytes 1574408 | tf_op jit(solution)/shard_map/ppermute | solution.py:27
  71.8 27.3 %collective-permute-start.5 = (f32[2,2,100,328]{3,2,1,0:T(8,128)}, f32[2,2,100,328]{3,2,1,0:T(8,128)}, u32[]{:S(2)}, u32[]{:S(2)}) collective-permute-start(f32[2,2,100,328]{3,2,1,0:T(8,128)} %get-tuple-element.148), channel_id=1, source_target_pairs={{8,0},{16,8},{24,16},{9,1},{17,9},{25,17},{10,2},{18,10},{26,18},{... | collective-permute-start | bytes 1574408 | tf_op jit(solution)/shard_map/ppermute | solution.py:27
  102.0 13.7 %copy-start.2 = (f32[128,128]{1,0:T(8,128)S(1)}, f32[128,128]{1,0:T(8,128)}, u32[]{:S(2)}) copy-start(f32[128,128]{1,0:T(8,128)} %param.19) | copy-start | bytes 196612
  102.0 7.7 %collective-permute-start.6 = (f32[2,2,128,100]{3,2,1,0:T(8,128)S(1)}, f32[2,2,128,100]{3,2,1,0:T(8,128)S(1)}, u32[]{:S(2)}, u32[]{:S(2)}) collective-permute-start(f32[2,2,128,100]{3,2,1,0:T(8,128)S(1)} %get-tuple-element.183), channel_id=1, source_target_pairs={{0,1},{1,2},{2,3},{3,4},{4,5},{5,6},{6,7},{8,9},{9,10},{10,11},{11... | collective-permute-start | bytes 614408 | tf_op jit(solution)/shard_map/ppermute | solution.py:27
  106.5 7.7 %collective-permute-start.7 = (f32[2,2,128,100]{3,2,1,0:T(8,128)S(1)}, f32[2,2,128,100]{3,2,1,0:T(8,128)S(1)}, u32[]{:S(2)}, u32[]{:S(2)}) collective-permute-start(f32[2,2,128,100]{3,2,1,0:T(8,128)S(1)} %get-tuple-element.182), channel_id=1, source_target_pairs={{1,0},{2,1},{3,2},{4,3},{5,4},{6,5},{7,6},{9,8},{10,9},{11,10},{12... | collective-permute-start | bytes 614408 | tf_op jit(solution)/shard_map/ppermute | solution.py:27
  115.7 2.6 %collective-permute-start.8 = (f32[5,3,128]{2,1,0:T(4,128)S(1)}, f32[5,3,128]{2,1,0:T(4,128)S(1)}, u32[]{:S(2)}, u32[]{:S(2)}) collective-permute-start(f32[5,3,128]{2,1,0:T(4,128)S(1)} %get-tuple-element.189), channel_id=1, source_target_pairs={{0,8},{8,16},{16,24},{1,9},{9,17},{17,25},{2,10},{10,18},{18,26},{... | collective-permute-start | bytes 23048 | tf_op jit(solution)/shard_map/ppermute | solution.py:37
  117.0 4.4 %collective-permute-start.9 = (f32[5,3,128]{2,1,0:T(4,128)S(1)}, f32[5,3,128]{2,1,0:T(4,128)S(1)}, u32[]{:S(2)}, u32[]{:S(2)}) collective-permute-start(f32[5,3,128]{2,1,0:T(4,128)S(1)} %get-tuple-element.190), channel_id=1, source_target_pairs={{8,0},{16,8},{24,16},{9,1},{17,9},{25,17},{10,2},{18,10},{26,18},{... | collective-permute-start | bytes 23048 | tf_op jit(solution)/shard_map/ppermute | solution.py:38
  121.6 7.3 %collective-permute-start.10 = (f32[5,134,3]{2,1,0:T(8,128)S(1)}, f32[5,134,3]{2,1,0:T(8,128)S(1)}, u32[]{:S(2)}, u32[]{:S(2)}) collective-permute-start(f32[5,134,3]{2,1,0:T(8,128)S(1)} %get-tuple-element.187), channel_id=1, source_target_pairs={{0,1},{1,2},{2,3},{3,4},{4,5},{5,6},{6,7},{8,9},{9,10},{10,11},{11... | collective-permute-start | bytes 24128 | tf_op jit(solution)/shard_map/ppermute | solution.py:37
  124.7 8.6 %collective-permute-start.11 = (f32[5,134,3]{2,1,0:T(8,128)S(1)}, f32[5,134,3]{2,1,0:T(8,128)S(1)}, u32[]{:S(2)}, u32[]{:S(2)}) collective-permute-start(f32[5,134,3]{2,1,0:T(8,128)S(1)} %get-tuple-element.188), channel_id=1, source_target_pairs={{1,0},{2,1},{3,2},{4,3},{5,4},{6,5},{7,6},{9,8},{10,9},{11,10},{12... | collective-permute-start | bytes 24128 | tf_op jit(solution)/shard_map/ppermute | solution.py:38
where the time goes:
time: 140 us; the launch traced here: 138 us
  waiting for transfers between devices  46.6 us (33%)
  local copies, waits for them, and re-layouts  31.2 us (22%)
  starting transfers between devices  29.1 us (21%)
  other arithmetic  14.2 us (10%)
  matrix products  12.6 us (9%)
  between operations  4.54 us (3%)
    ppermute x4, waiting for transfers between devices, passed_along(): lax.ppermute(value, axis, [(source, source + steps) for source in range(f...  26.9 us
    ppermute x4, waiting for transfers between devices, padded(): after = lax.ppermute(first, axis, down)  15.5 us
    dynamic_update_slice x1, local copies, waits for them, and re-layouts, add_view(): return lax.dynamic_update_slice(summed, current + gradient, place)  14.3 us
    ppermute x4, starting transfers between devices, padded(): before = lax.ppermute(last, axis, up)  12.2 us
    ppermute x4, starting transfers between devices, passed_along(): lax.ppermute(value, axis, [(source, source + steps) for source in range(f...  10.2 us
    ppermute x4, starting transfers between devices, padded(): after = lax.ppermute(first, axis, down)  6.67 us
    dot_general x6, matrix products, transform(): jnp.dot(jnp.concatenate([cosine, sine], axis=0), jnp.concatenate([real_in...  6.38 us
    dot_general x6, matrix products, transform(): jnp.dot(jnp.concatenate([left_real, left_imag], axis=0), jnp.concatenate(...  6.23 us
  transfers between devices with their start and end apart: 12, of which 10 were waited for; matrix products, arithmetic and copies ran while one was open for 8% of the time, Pallas kernels for 0%

commit v1 on v0

v1 whole, which is shorter than its diff:
```python
import functools
import math

import jax
import jax.numpy as jnp
import numpy as np
from jax import lax
from jax.experimental import pallas as pl
from jax.experimental.pallas import tpu as pltpu
from jax.sharding import PartitionSpec as P

MESH = pl.DeviceIdType.MESH
F32, BF16 = jnp.float32, jnp.bfloat16
CORE = 128
PROBE = 256
HALF = 128
BAND = 104
ROWS = BAND + CORE + BAND
COLS = 3 * CORE
HALO = 100
REACH = 3
TVROWS = 136
UPROWS = 112
AMP_EPS = 0.1
LEARN_RATE = 0.2
TV_EPS = 1.0
TV_TAU = 0.1
TV_STEPS = 3


def tables():
    k, j = np.arange(HALF)[:, None], np.arange(HALF)[None, :]
    parts = []
    for odd in (0, 1):
        angle = 2.0 * np.pi * (((2 * k + odd) * j) % PROBE) / PROBE
        c, s = np.cos(angle) / math.sqrt(PROBE), np.sin(angle) / math.sqrt(PROBE)
        full = np.block([[c, s], [-s, c]])
        parts.append(full)
    out = []
    for full in (parts[0], parts[0].T, parts[1], parts[1].T):
        full = full.astype(np.float32)
        high = full.astype(BF16)
        out += [high, (full - high.astype(np.float32)).astype(BF16)]
    order = np.zeros((PROBE, PROBE), np.float32)
    order[np.arange(HALF), 2 * np.arange(HALF)] = 1
    order[HALF + np.arange(HALF), 2 * np.arange(HALF) + 1] = 1
    out += [order.astype(BF16), order.T.astype(BF16)]
    return np.stack(out)


def split(x):
    high = x.astype(BF16)
    return high, (x - high.astype(F32)).astype(BF16)


def mm(a, b):
    return jnp.dot(a, b, preferred_element_type=F32)


def left(tab, i, x):
    wh, wl = tab[2 * i], tab[2 * i + 1]
    xh, xl = split(x)
    return mm(wh, xh) + (mm(wh, xl) + mm(wl, xh))


def right(tab, i, x):
    wh, wl = tab[2 * i], tab[2 * i + 1]
    xh, xl = split(x)
    return mm(xh, wh) + (mm(xl, wh) + mm(xh, wl))


def cat(a, b, axis):
    return jnp.concatenate([a, b], axis=axis)


def forward(tab, re, im):
    h = HALF
    e = left(tab, 0, cat(re[:h] + re[h:], im[:h] + im[h:], 0))
    o = left(tab, 2, cat(re[:h] - re[h:], im[:h] - im[h:], 0))
    re, im = cat(e[:h], o[:h], 0), cat(e[h:], o[h:], 0)
    e = right(tab, 1, cat(re[:, :h] + re[:, h:], im[:, :h] + im[:, h:], 1))
    o = right(tab, 3, cat(re[:, :h] - re[:, h:], im[:, :h] - im[:, h:], 1))
    return cat(e[:, :h], o[:, :h], 1), cat(e[:, h:], o[:, h:], 1)


def inverse(tab, re, im):
    h = HALF
    e = left(tab, 1, cat(re[:h], im[:h], 0))
    o = left(tab, 3, cat(re[h:], im[h:], 0))
    s, d = e + o, e - o
    re, im = cat(s[:h], d[:h], 0), cat(s[h:], d[h:], 0)
    e = right(tab, 0, cat(re[:, :h], im[:, :h], 1))
    o = right(tab, 2, cat(re[:, h:], im[:, h:], 1))
    s, d = e + o, e - o
    return cat(s[:, :h], d[:, :h], 1), cat(s[:, h:], d[:, h:], 1)


def reorder(tab, x):
    for axis in (0, 1):
        total = None
        rest = x
        for _ in range(3):
            part = rest.astype(BF16)
            rest = rest - part.astype(F32)
            term = mm(tab[8], part) if axis == 0 else mm(part, tab[9])
            total = term if total is None else total + term
        x = total
    return x


class Place:
    def __init__(self):
        self.r, self.c = lax.axis_index("row"), lax.axis_index("col")
        nr, nc = lax.axis_size("row"), lax.axis_size("col")
        self.has = {"up": self.r > 0, "down": self.r < nr - 1, "left": self.c > 0, "right": self.c < nc - 1}
        self.to = {"up": {"row": self.r - 1}, "down": {"row": self.r + 1}, "left": {"col": self.c - 1}, "right": {"col": self.c + 1}}

    def barrier(self):
        sem = pltpu.get_barrier_semaphore()
        for side in OPPOSITE:
            @pl.when(self.has[side])
            def _():
                pl.semaphore_signal(sem, inc=1, device_id=self.to[side], device_id_type=MESH)
        pl.semaphore_wait(sem, sum(self.has[side].astype(jnp.int32) for side in OPPOSITE))


OPPOSITE = {"up": "down", "down": "up", "left": "right", "right": "left"}


class Copy:
    def __init__(self, place, side, src, dst, sems, i, also=None):
        self.op = pltpu.make_async_remote_copy(
            src_ref=src, dst_ref=dst, send_sem=sems[0].at[i], recv_sem=sems[1].at[i],
            device_id=place.to[side], device_id_type=MESH,
        )
        self.sends, self.gets = place.has[side], place.has[OPPOSITE[side]]
        if also is not None:
            self.sends, self.gets = self.sends & also, self.gets & also

    def start(self):
        pl.when(self.sends)(lambda: self.op.start())

    def got(self):
        pl.when(self.gets)(lambda: self.op.wait_recv())

    def sent(self):
        pl.when(self.sends)(lambda: self.op.wait_send())


def exchange_kernel(tr, w, ext, wext, send, recv):
    place = Place()
    has = place.has
    sems = (send, recv)
    place.barrier()
    mid = pl.ds(CORE, CORE)
    lanes = {"left": pl.ds(2 * CORE, CORE), "right": pl.ds(0, CORE)}
    jobs = []
    for ch in range(5):
        band = BAND if ch < 4 else 8
        src = tr.at[ch] if ch < 4 else w
        dst = ext.at[ch] if ch < 4 else wext
        jobs.append((band, src, dst))
    copies, corners = [], []
    for ch, (band, src, dst) in enumerate(jobs):
        base = 8 * ch
        top, low = pl.ds(0, band), pl.ds(band + CORE, band)
        group = [
            Copy(place, "up", src.at[pl.ds(0, band)], dst.at[low, mid], sems, base),
            Copy(place, "down", src.at[pl.ds(CORE - band, band)], dst.at[top, mid], sems, base + 1),
            Copy(place, "left", src, dst.at[pl.ds(band, CORE), lanes["left"]], sems, base + 2),
            Copy(place, "right", src, dst.at[pl.ds(band, CORE), lanes["right"]], sems, base + 3),
        ]
        for c in group:
            c.start()
        copies.append(group)
        corner = []
        for n, (rows, there) in enumerate(((low, has["down"]), (top, has["up"]))):
            for m, side in enumerate(("left", "right")):
                corner.append(Copy(place, side, dst.at[rows, mid], dst.at[rows, lanes[side]], sems, base + 4 + 2 * n + m, there))
        corners.append(corner)
    for (band, src, dst) in jobs:
        dst[band : band + CORE, CORE : 2 * CORE] = src[...]
        total = dst.shape[0]

        @pl.when(jnp.logical_not(has["up"]))
        def _():
            dst[0:band, :] = jnp.zeros((band, COLS), F32)

        @pl.when(jnp.logical_not(has["down"]))
        def _():
            dst[band + CORE : total, :] = jnp.zeros((band, COLS), F32)

        @pl.when(jnp.logical_not(has["left"]))
        def _():
            dst[:, 0:CORE] = jnp.zeros((total, CORE), F32)

        @pl.when(jnp.logical_not(has["right"]))
        def _():
            dst[:, 2 * CORE :] = jnp.zeros((total, CORE), F32)
    for ch in range(5):
        for n in (0, 1):
            copies[ch][n].got()
            for m in (0, 1):
                corners[ch][2 * n + m].start()
    for ch in range(5):
        for c in copies[ch][2:] + corners[ch]:
            c.got()
        for c in copies[ch] + corners[ch]:
            c.sent()


def view_kernel(pos, ext, probe, phase, amp, tab, own, lband):
    p, q = pos[0], pos[1]

    def window(ch):
        rows = pltpu.roll(ext[ch], ROWS - (BAND - HALO) - p, 0)[:PROBE]
        return pltpu.roll(rows, COLS - (q + (CORE - HALO)), 1)[:, :PROBE]

    def put(ch, grad):
        wide = cat(grad, jnp.zeros((PROBE, COLS - PROBE), F32), 1)
        wide = cat(wide, jnp.zeros((ROWS - PROBE, COLS), F32), 0)
        wide = pltpu.roll(wide, p + (BAND + REACH - HALO), 0)
        at_own = lax.rem(q + (COLS - HALO + REACH), COLS)
        own[ch] = pltpu.roll(wide, at_own, 1)[:, :PROBE]
        lband[ch] = pltpu.roll(wide, q + (CORE - REACH - HALO), 1)[:, :CORE]

    phase = reorder(tab, phase[...])
    kr, ki = jnp.cos(phase), jnp.sin(phase)
    measured = reorder(tab, amp[...])
    ar, ai = window(0), window(1)
    br, bi = window(2), window(3)
    pr, pi = probe[0], probe[1]
    fr, fi = forward(tab, ar * pr - ai * pi, ar * pi + ai * pr)
    wr, wi = inverse(tab, kr * fr - ki * fi, kr * fi + ki * fr)
    fr, fi = forward(tab, br * wr - bi * wi, br * wi + bi * wr)
    factor = 1.0 - measured / jnp.sqrt(fr * fr + fi * fi + AMP_EPS)
    gr, gi = inverse(tab, fr * factor, fi * factor)
    put(2, wr * gr + wi * gi)
    put(3, wr * gi - wi * gr)
    fr, fi = forward(tab, br * gr + bi * gi, br * gi - bi * gr)
    gr, gi = inverse(tab, kr * fr + ki * fi, kr * fi - ki * fr)
    put(0, pr * gr + pi * gi)
    put(1, pr * gi - pi * gr)


def fold_kernel(own, lband, ext, wext, out, from_left, from_right, total, from_up, from_down, send, recv):
    place = Place()
    has = place.has
    sems = (send, recv)
    place.barrier()
    order = (2, 3, 0, 1)
    across = {}
    for ch in order:
        across[ch] = (
            Copy(place, "right", own.at[ch, :, pl.ds(CORE, CORE)], from_left.at[ch], sems, 2 * ch),
            Copy(place, "left", lband.at[ch], from_right.at[ch], sems, 2 * ch + 1),
        )
        for c in across[ch]:
            c.start()

    for side, ref in (("left", from_left), ("right", from_right), ("up", from_up), ("down", from_down)):
        @pl.when(jnp.logical_not(has[side]))
        def _():
            ref[...] = jnp.zeros(ref.shape, F32)

    lane = lax.broadcasted_iota(jnp.int32, (ROWS, CORE), 1)
    packed = jnp.zeros((ROWS, CORE), F32)
    along = []
    for n, ch in enumerate(order + (4,)):
        if ch < 4:
            for c in across[ch]:
                c.got()
            shifted = pltpu.roll(from_right[ch], 2 * REACH, 1)
            total[ch] = own[ch, :, :CORE] + from_left[ch] + jnp.where(lane >= 2 * REACH, shifted, 0.0)
            rest = jnp.where(lane < 2 * REACH, own[ch, :, CORE:] + shifted, 0.0)
            packed = packed + (pltpu.roll(rest, 8 * ch, 1) if ch else rest)
        else:
            total[4] = packed
        pair = (
            Copy(place, "down", total.at[ch, pl.ds(ROWS - BAND, BAND)], from_up.at[ch], sems, 8 + 2 * ch),
            Copy(place, "up", total.at[ch, pl.ds(0, UPROWS)], from_down.at[ch], sems, 9 + 2 * ch),
        )
        for c in pair:
            c.start()
        along.append(pair)

    grad = {}
    for pair, ch in zip(along, order + (4,)):
        for c in pair:
            c.got()
        mine = total[ch, BAND : BAND + TVROWS, :]
        upper = cat(from_up[ch], jnp.zeros((TVROWS - BAND, CORE), F32), 0)
        lower = cat(jnp.zeros((TVROWS - UPROWS, CORE), F32), from_down[ch], 0)
        grad[ch] = mine + upper + lower

    shape = (TVROWS, PROBE)
    row_at = lax.broadcasted_iota(jnp.int32, shape, 0) - REACH + place.r * CORE
    col_at = lax.broadcasted_iota(jnp.int32, shape, 1) - REACH + place.c * CORE
    inside = (row_at >= 0) & (row_at < lax.axis_size("row") * CORE) & (col_at >= 0) & (col_at < lax.axis_size("col") * CORE)
    inside = inside.astype(F32)

    def cut(ref_rows):
        return pltpu.roll(ref_rows, COLS - (CORE - REACH), 1)[:, :PROBE]

    weight = cut(wext[8 - REACH : 8 - REACH + TVROWS, :]) * inside
    fields = []
    for ch in range(4):
        rest = pltpu.roll(grad[4], CORE - 8 * ch, 1) if ch else grad[4]
        field = cut(ext[ch, BAND - REACH : BAND - REACH + TVROWS, :])
        fields.append((field - LEARN_RATE * cat(grad[ch], rest, 1)) * inside)
    for s in range(2):
        pair = fields[2 * s : 2 * s + 2]
        for _ in range(TV_STEPS):
            down = [pltpu.roll(f, TVROWS - 1, 0) - f for f in pair]
            along_row = [pltpu.roll(f, PROBE - 1, 1) - f for f in pair]
            square = down[0] * down[0] + along_row[0] * along_row[0] + (down[1] * down[1] + along_row[1] * along_row[1])
            gain = weight / jnp.sqrt(square + TV_EPS)
            fresh = []
            for f, d, r in zip(pair, down, along_row):
                d, r = gain * d, gain * r
                update = d - pltpu.roll(d, 1, 0) + (r - pltpu.roll(r, 1, 1))
                fresh.append((f + TV_TAU * update) * inside)
            pair = fresh
        for c in range(2):
            out[2 * s + c] = pltpu.roll(pair[c], PROBE - REACH, 1)[REACH : REACH + CORE, :CORE]
    for ch in order:
        for c in across[ch]:
            c.sent()
    for pair in along:
        for c in pair:
            c.sent()


def spec():
    return pl.BlockSpec(memory_space=pltpu.VMEM)


def shape_of(*dims):
    return jax.ShapeDtypeStruct(dims, F32)


def body(transmission, probe, fresnel_phase, amplitudes, positions, tv_weight):
    tr = transmission.reshape(4, CORE, CORE)
    tab = jnp.asarray(tables())
    ext, wext = pl.pallas_call(
        exchange_kernel,
        out_shape=(shape_of(4, ROWS, COLS), shape_of(CORE + 16, COLS)),
        in_specs=[spec()] * 2,
        out_specs=(spec(), spec()),
        scratch_shapes=[pltpu.SemaphoreType.DMA((40,)), pltpu.SemaphoreType.DMA((40,))],
        compiler_params=pltpu.CompilerParams(collective_id=0, has_side_effects=True),
        name="exchange",
    )(tr, tv_weight)
    own, lband = pl.pallas_call(
        view_kernel,
        out_shape=(shape_of(4, ROWS, PROBE), shape_of(4, ROWS, CORE)),
        in_specs=[pl.BlockSpec(memory_space=pltpu.SMEM)] + [spec()] * 5,
        out_specs=(spec(), spec()),
        name="view",
    )(positions.reshape(2), ext, probe, fresnel_phase, amplitudes.reshape(PROBE, PROBE), tab)
    out = pl.pallas_call(
        fold_kernel,
        out_shape=shape_of(4, CORE, CORE),
        in_specs=[spec()] * 4,
        out_specs=spec(),
        scratch_shapes=[
            pltpu.VMEM((4, ROWS, CORE), F32),
            pltpu.VMEM((4, ROWS, CORE), F32),
            pltpu.VMEM((5, ROWS, CORE), F32),
            pltpu.VMEM((5, BAND, CORE), F32),
            pltpu.VMEM((5, UPROWS, CORE), F32),
            pltpu.SemaphoreType.DMA((18,)),
            pltpu.SemaphoreType.DMA((18,)),
        ],
        compiler_params=pltpu.CompilerParams(collective_id=1, has_side_effects=True),
        name="fold",
    )(own, lband, ext, wext)
    return out.reshape(2, 2, CORE, CORE)


def solution(mesh):
    placed = (
        P(None, None, "row", "col"),
        P(),
        P(),
        P("row", "col", None, None, None),
        P("row", "col", None, None),
        P("row", "col"),
    )
    return jax.shard_map(
        body, mesh=mesh, in_specs=placed, out_specs=P(None, None, "row", "col"), check_vma=False
    )
```

time: 140 us -> 57.5 us (0.41); the launches traced: 138 us -> 57.3 us
  Pallas kernels: 0 us -> 55.6 us
  waiting for transfers between devices: 46.6 us -> 0 us
  local copies, waits for them, and re-layouts: 31.2 us -> 1.67 us
  starting transfers between devices: 29.1 us -> 0 us
  other arithmetic: 14.2 us -> 0 us
  matrix products: 12.6 us -> 0 us
  between operations: 4.54 us -> 0.02 us
    pallas_call x0 -> x3, Pallas kernels: none -> 55.6 us  [the longest x1 25.6 us: body(): pl.pallas_call(fold_kernel, out_shape=shape_of(4, CORE, CORE), in_specs=[...]
    ppermute x12 -> x0, waiting for transfers between devices: 46.6 us -> none  [the longest x4 26.9 us: passed_along(): lax.ppermute(value, axis, [(source, source + steps) for source in range(f...]
    ppermute x12 -> x0, starting transfers between devices: 29.1 us -> none  [the longest x4 12.2 us: padded(): before = lax.ppermute(last, axis, up)]
    dynamic_update_slice x1 -> x0, local copies, waits for them, and re-layouts: 14.3 us -> none  [add_view(): return lax.dynamic_update_slice(summed, current + gradient, place)]
    dot_general x12 -> x0, matrix products: 12.6 us -> none  [the longest x6 6.38 us: transform(): jnp.dot(jnp.concatenate([cosine, sine], axis=0), jnp.concatenate([real_in...]
    scatter-add x4 -> x0, local copies, waits for them, and re-layouts: 6.61 us -> none  [the longest x1 3.28 us: fold_rows(): kept = kept.at[:, :, :HALO, :].add(arrived)]
    slice x15 -> x0, local copies, waits for them, and re-layouts: 5.2 us -> none  [the longest x4 1.8 us: padded(): last = lax.slice_in_dim(value, length - width, length, axis=dim)]
    mul x8 -> x0, other arithmetic: 3.87 us -> none  [the longest x3 2.4 us: tv_update(): return (field[:, :, 1:-1, 1:-1] + TV_TAU * update) * inside[1:-1, 1:-1]]
  transfers between devices with their start and end apart: 12 -> 0, of which waited for: 10 -> 0; matrix products, arithmetic and copies ran while one was open for 8% -> 0% of each run, Pallas kernels for 0% -> 0%
where the time goes in v1:
time: 57.5 us; the launch traced here: 57.3 us
  Pallas kernels  55.6 us (97%)
  local copies, waits for them, and re-layouts  1.67 us (3%)
    pallas_call x1, Pallas kernels, body(): pl.pallas_call(fold_kernel, out_shape=shape_of(4, CORE, CORE), in_specs=[...  25.6 us
    pallas_call x1, Pallas kernels, body(): pl.pallas_call(exchange_kernel, out_shape=(shape_of(4, ROWS, COLS), shape...  19.5 us
    pallas_call x1, Pallas kernels, body(): pl.pallas_call(view_kernel, out_shape=(shape_of(4, ROWS, PROBE), shape_of...  10.5 us
    unnamed x1, local copies, waits for them, and re-layouts  1.67 us

profile of v1, /device:TPU:9, one launch (start us, length us, event | category | flops | bytes accessed | tf_op | source)
XLA Modules:
  0.0 57.3 jit_solution(9883838505838458694)
XLA Ops:
  0.0 19.5 %exchange.1 = (f32[4,336,384]{2,1,0:T(8,128)}, f32[144,384]{1,0:T(8,128)}) custom-call(f32[4,128,128]{2,1,0:T(8,128)} %bitcast.6, f32[128,128]{1,0:T(8,128)} %w.1), custom_call_target="tpu_custom_call" | custom-call | tf_op jit(solution)/shard_map/exchange/pallas_call | solution.py:345
  19.5 10.5 %view.1 = (f32[4,336,256]{2,1,0:T(8,128)}, f32[4,336,128]{2,1,0:T(8,128)}) custom-call(s32[2]{0:T(128)} %bitcast.7, f32[4,336,384]{2,1,0:T(8,128)} %get-tuple-element.9.ext, f32[2,256,256]{2,1,0:T(8,128)} %probe.1, f32[256,256]{1,0:T(8,128)} %phase.1, f32[256,256]{1,0:T(8,128)} %bitcast.5, bf16[10,256,256]{2,1,0:T(8,128)(2,1)} %constant.2.clone.tab), custom_call_target="tpu_custom_call" | custom-call | tf_op jit(solution)/shard_map/view/pallas_call | solution.py:354
  30.0 25.6 %fold.1 = f32[4,128,128]{2,1,0:T(8,128)} custom-call(f32[4,336,256]{2,1,0:T(8,128)} %get-tuple-element.10.own, f32[4,336,128]{2,1,0:T(8,128)} %get-tuple-element.11.lband, f32[4,336,384]{2,1,0:T(8,128)} %get-tuple-element.9.ext, f32[144,384]{1,0:T(8,128)} %get-tuple-element.12.wext), custom_call_target="tpu_custom_call" | custom-call | tf_op jit(solution)/shard_map/fold/pallas_call | solution.py:361
  55.7 1.7 %copy.9 = f32[2,2,128,128]{3,2,1,0:T(8,128)} copy(f32[2,2,128,128]{3,2,1,0:T(8,128)} %bitcast.4) | data formatting | bytes 524288

commit v2 on v1

--- a/solution.py
+++ b/solution.py
@@ -147,19 +147,23 @@
         pl.when(self.sends)(lambda: self.op.wait_send())
 
 
-def exchange_kernel(tr, w, ext, wext, send, recv):
+def whole_kernel(
+    pos, tr, w, probe_any, phase_any, amp_any, tab_any, out,
+    probe, phase_ref, amp, tab, ext, wext, own, lband, from_left, from_right,
+    total, pack, from_up, from_down, pack_up, pack_down, send, recv, local,
+):
     place = Place()
     has = place.has
     sems = (send, recv)
+    loads = []
+    for n, (src, dst) in enumerate(((phase_any, phase_ref), (amp_any, amp), (tab_any, tab), (probe_any, probe))):
+        load = pltpu.make_async_copy(src, dst, local.at[n])
+        load.start()
+        loads.append(load)
     place.barrier()
     mid = pl.ds(CORE, CORE)
     lanes = {"left": pl.ds(2 * CORE, CORE), "right": pl.ds(0, CORE)}
-    jobs = []
-    for ch in range(5):
-        band = BAND if ch < 4 else 8
-        src = tr.at[ch] if ch < 4 else w
-        dst = ext.at[ch] if ch < 4 else wext
-        jobs.append((band, src, dst))
+    jobs = [(BAND, tr.at[ch], ext.at[ch]) for ch in range(4)] + [(8, w, wext)]
     copies, corners = [], []
     for ch, (band, src, dst) in enumerate(jobs):
         base = 8 * ch
@@ -178,9 +182,22 @@
             for m, side in enumerate(("left", "right")):
                 corner.append(Copy(place, side, dst.at[rows, mid], dst.at[rows, lanes[side]], sems, base + 4 + 2 * n + m, there))
         corners.append(corner)
+
+    def forward_corners(channels):
+        for ch in channels:
+            for n in (0, 1):
+                copies[ch][n].got()
+                for m in (0, 1):
+                    corners[ch][2 * n + m].start()
+
+    def arrived(channels):
+        for ch in channels:
+            for c in copies[ch][2:] + corners[ch]:
+                c.got()
+
     for (band, src, dst) in jobs:
         dst[band : band + CORE, CORE : 2 * CORE] = src[...]
-        total = dst.shape[0]
+        rows = dst.shape[0]
 
         @pl.when(jnp.logical_not(has["up"]))
         def _():
@@ -188,111 +205,111 @@
 
         @pl.when(jnp.logical_not(has["down"]))
         def _():
-            dst[band + CORE : total, :] = jnp.zeros((band, COLS), F32)
+            dst[band + CORE : rows, :] = jnp.zeros((band, COLS), F32)
 
         @pl.when(jnp.logical_not(has["left"]))
         def _():
-            dst[:, 0:CORE] = jnp.zeros((total, CORE), F32)
+            dst[:, 0:CORE] = jnp.zeros((rows, CORE), F32)
 
         @pl.when(jnp.logical_not(has["right"]))
         def _():
-            dst[:, 2 * CORE :] = jnp.zeros((total, CORE), F32)
-    for ch in range(5):
-        for n in (0, 1):
-            copies[ch][n].got()
-            for m in (0, 1):
-                corners[ch][2 * n + m].start()
-    for ch in range(5):
-        for c in copies[ch][2:] + corners[ch]:
-            c.got()
-        for c in copies[ch] + corners[ch]:
-            c.sent()
-
-
-def view_kernel(pos, ext, probe, phase, amp, tab, own, lband):
+            dst[:, 2 * CORE :] = jnp.zeros((rows, CORE), F32)
+    edges = (
+        ("left", from_left), ("right", from_right), ("up", from_up), ("down", from_down),
+        ("up", pack_up), ("down", pack_down),
+    )
+    for side, ref in edges:
+        @pl.when(jnp.logical_not(has[side]))
+        def _():
+            ref[...] = jnp.zeros(ref.shape, F32)
+
     p, q = pos[0], pos[1]
 
     def window(ch):
         rows = pltpu.roll(ext[ch], ROWS - (BAND - HALO) - p, 0)[:PROBE]
         return pltpu.roll(rows, COLS - (q + (CORE - HALO)), 1)[:, :PROBE]
 
+    across = {}
+
     def put(ch, grad):
         wide = cat(grad, jnp.zeros((PROBE, COLS - PROBE), F32), 1)
-        wide = cat(wide, jnp.zeros((ROWS - PROBE, COLS), F32), 0)
-        wide = pltpu.roll(wide, p + (BAND + REACH - HALO), 0)
         at_own = lax.rem(q + (COLS - HALO + REACH), COLS)
-        own[ch] = pltpu.roll(wide, at_own, 1)[:, :PROBE]
-        lband[ch] = pltpu.roll(wide, q + (CORE - REACH - HALO), 1)[:, :CORE]
-
-    phase = reorder(tab, phase[...])
+        below = jnp.zeros((ROWS - PROBE, PROBE), F32)
+        down_by = p + (BAND + REACH - HALO)
+        own[ch] = pltpu.roll(cat(pltpu.roll(wide, at_own, 1)[:, :PROBE], below, 0), down_by, 0)
+        turned = pltpu.roll(wide, q + (CORE - REACH - HALO), 1)[:, :CORE]
+        lband[ch] = pltpu.roll(cat(turned, below[:, :CORE], 0), down_by, 0)
+        across[ch] = (
+            Copy(place, "right", own.at[ch, :, pl.ds(CORE, CORE)], from_left.at[ch], sems, 40 + 2 * ch),
+            Copy(place, "left", lband.at[ch], from_right.at[ch], sems, 41 + 2 * ch),
+        )
+        for c in across[ch]:
+            c.start()
+
+    for load in loads[:3]:
+        load.wait()
+    phase = reorder(tab, phase_ref[...])
     kr, ki = jnp.cos(phase), jnp.sin(phase)
     measured = reorder(tab, amp[...])
+    loads[3].wait()
+    forward_corners((0, 1))
+    arrived((0, 1))
     ar, ai = window(0), window(1)
-    br, bi = window(2), window(3)
     pr, pi = probe[0], probe[1]
     fr, fi = forward(tab, ar * pr - ai * pi, ar * pi + ai * pr)
+    forward_corners((2, 3))
     wr, wi = inverse(tab, kr * fr - ki * fi, kr * fi + ki * fr)
+    arrived((2, 3))
+    forward_corners((4,))
+    br, bi = window(2), window(3)
     fr, fi = forward(tab, br * wr - bi * wi, br * wi + bi * wr)
     factor = 1.0 - measured / jnp.sqrt(fr * fr + fi * fi + AMP_EPS)
     gr, gi = inverse(tab, fr * factor, fi * factor)
     put(2, wr * gr + wi * gi)
     put(3, wr * gi - wi * gr)
+    along = []
+    lane = lax.broadcasted_iota(jnp.int32, (ROWS, CORE), 1)
+
+    def fold(ch):
+        for c in across[ch]:
+            c.got()
+        shifted = pltpu.roll(from_right[ch], 2 * REACH, 1)
+        total[ch] = own[ch, :, :CORE] + from_left[ch] + jnp.where(lane >= 2 * REACH, shifted, 0.0)
+        rest = jnp.where(lane < 2 * REACH, own[ch, :, CORE:] + shifted, 0.0)
+        pair = (
+            Copy(place, "down", total.at[ch, pl.ds(ROWS - BAND, BAND)], from_up.at[ch], sems, 48 + 2 * ch),
+            Copy(place, "up", total.at[ch, pl.ds(0, UPROWS)], from_down.at[ch], sems, 49 + 2 * ch),
+        )
+        for c in pair:
+            c.start()
+        along.append(pair)
+        return pltpu.roll(rest, 8 * ch, 1) if ch else rest
+
     fr, fi = forward(tab, br * gr + bi * gi, br * gi - bi * gr)
     gr, gi = inverse(tab, kr * fr + ki * fi, kr * fi - ki * fr)
     put(0, pr * gr + pi * gi)
     put(1, pr * gi - pi * gr)
-
-
-def fold_kernel(own, lband, ext, wext, out, from_left, from_right, total, from_up, from_down, send, recv):
-    place = Place()
-    has = place.has
-    sems = (send, recv)
-    place.barrier()
-    order = (2, 3, 0, 1)
-    across = {}
-    for ch in order:
-        across[ch] = (
-            Copy(place, "right", own.at[ch, :, pl.ds(CORE, CORE)], from_left.at[ch], sems, 2 * ch),
-            Copy(place, "left", lband.at[ch], from_right.at[ch], sems, 2 * ch + 1),
-        )
-        for c in across[ch]:
-            c.start()
-
-    for side, ref in (("left", from_left), ("right", from_right), ("up", from_up), ("down", from_down)):
-        @pl.when(jnp.logical_not(has[side]))
-        def _():
-            ref[...] = jnp.zeros(ref.shape, F32)
-
-    lane = lax.broadcasted_iota(jnp.int32, (ROWS, CORE), 1)
-    packed = jnp.zeros((ROWS, CORE), F32)
-    along = []
-    for n, ch in enumerate(order + (4,)):
-        if ch < 4:
-            for c in across[ch]:
-                c.got()
-            shifted = pltpu.roll(from_right[ch], 2 * REACH, 1)
-            total[ch] = own[ch, :, :CORE] + from_left[ch] + jnp.where(lane >= 2 * REACH, shifted, 0.0)
-            rest = jnp.where(lane < 2 * REACH, own[ch, :, CORE:] + shifted, 0.0)
-            packed = packed + (pltpu.roll(rest, 8 * ch, 1) if ch else rest)
-        else:
-            total[4] = packed
-        pair = (
-            Copy(place, "down", total.at[ch, pl.ds(ROWS - BAND, BAND)], from_up.at[ch], sems, 8 + 2 * ch),
-            Copy(place, "up", total.at[ch, pl.ds(0, UPROWS)], from_down.at[ch], sems, 9 + 2 * ch),
-        )
-        for c in pair:
-            c.start()
-        along.append(pair)
-
-    grad = {}
-    for pair, ch in zip(along, order + (4,)):
-        for c in pair:
-            c.got()
-        mine = total[ch, BAND : BAND + TVROWS, :]
-        upper = cat(from_up[ch], jnp.zeros((TVROWS - BAND, CORE), F32), 0)
-        lower = cat(jnp.zeros((TVROWS - UPROWS, CORE), F32), from_down[ch], 0)
-        grad[ch] = mine + upper + lower
-
+    packed = fold(2) + fold(3) + fold(0) + fold(1)
+
+    def compact(rows):
+        rows = cat(rows, jnp.zeros((CORE - rows.shape[0], CORE), F32), 0)
+        parts = [rows[32 * k : 32 * k + 32] for k in range(4)]
+        return parts[0] + sum(pltpu.roll(parts[k], 32 * k, 1) for k in (1, 2, 3))
+
+    def spread_out(x):
+        return jnp.concatenate([x] + [pltpu.roll(x, CORE - 32 * k, 1) for k in (1, 2, 3)], axis=0)
+
+    pack[0] = compact(packed[ROWS - BAND :])
+    pack[1] = compact(packed[:UPROWS])
+    pair = (
+        Copy(place, "down", pack.at[0], pack_up, sems, 56),
+        Copy(place, "up", pack.at[1], pack_down, sems, 57),
+    )
+    for c in pair:
+        c.start()
+    along.append(pair)
+
+    arrived((4,))
     shape = (TVROWS, PROBE)
     row_at = lax.broadcasted_iota(jnp.int32, shape, 0) - REACH + place.r * CORE
     col_at = lax.broadcasted_iota(jnp.int32, shape, 1) - REACH + place.c * CORE
@@ -303,11 +320,22 @@
         return pltpu.roll(ref_rows, COLS - (CORE - REACH), 1)[:, :PROBE]
 
     weight = cut(wext[8 - REACH : 8 - REACH + TVROWS, :]) * inside
+    for pair in along:
+        for c in pair:
+            c.got()
+
+    def joined(mine, upper, lower):
+        upper = cat(upper, jnp.zeros((TVROWS - BAND, CORE), F32), 0)
+        lower = cat(jnp.zeros((TVROWS - UPROWS, CORE), F32), lower, 0)
+        return mine[BAND : BAND + TVROWS] + upper + lower
+
+    side = joined(packed, spread_out(pack_up[...])[:BAND], spread_out(pack_down[...])[:UPROWS])
     fields = []
     for ch in range(4):
-        rest = pltpu.roll(grad[4], CORE - 8 * ch, 1) if ch else grad[4]
+        grad = joined(total[ch], from_up[ch], from_down[ch])
+        rest = pltpu.roll(side, CORE - 8 * ch, 1) if ch else side
         field = cut(ext[ch, BAND - REACH : BAND - REACH + TVROWS, :])
-        fields.append((field - LEARN_RATE * cat(grad[ch], rest, 1)) * inside)
+        fields.append((field - LEARN_RATE * cat(grad, rest, 1)) * inside)
     for s in range(2):
         pair = fields[2 * s : 2 * s + 2]
         for _ in range(TV_STEPS):
@@ -323,58 +351,46 @@
             pair = fresh
         for c in range(2):
             out[2 * s + c] = pltpu.roll(pair[c], PROBE - REACH, 1)[REACH : REACH + CORE, :CORE]
-    for ch in order:
-        for c in across[ch]:
+    for group in copies + corners + [across[ch] for ch in range(4)] + along:
+        for c in group:
             c.sent()
-    for pair in along:
-        for c in pair:
-            c.sent()
-
-
-def spec():
-    return pl.BlockSpec(memory_space=pltpu.VMEM)
-
-
-def shape_of(*dims):
-    return jax.ShapeDtypeStruct(dims, F32)
 
 
 def body(transmission, probe, fresnel_phase, amplitudes, positions, tv_weight):
-    tr = transmission.reshape(4, CORE, CORE)
-    tab = jnp.asarray(tables())
-    ext, wext = pl.pallas_call(
-        exchange_kernel,
-        out_shape=(shape_of(4, ROWS, COLS), shape_of(CORE + 16, COLS)),
-        in_specs=[spec()] * 2,
-        out_specs=(spec(), spec()),
-        scratch_shapes=[pltpu.SemaphoreType.DMA((40,)), pltpu.SemaphoreType.DMA((40,))],
-        compiler_params=pltpu.CompilerParams(collective_id=0, has_side_effects=True),
-        name="exchange",
-    )(tr, tv_weight)
-    own, lband = pl.pallas_call(
-        view_kernel,
-        out_shape=(shape_of(4, ROWS, PROBE), shape_of(4, ROWS, CORE)),
-        in_specs=[pl.BlockSpec(memory_space=pltpu.SMEM)] + [spec()] * 5,
-        out_specs=(spec(), spec()),
-        name="view",
-    )(positions.reshape(2), ext, probe, fresnel_phase, amplitudes.reshape(PROBE, PROBE), tab)
+    vmem, anywhere = (pl.BlockSpec(memory_space=m) for m in (pltpu.VMEM, pl.ANY))
+    tab = tables()
     out = pl.pallas_call(
-        fold_kernel,
-        out_shape=shape_of(4, CORE, CORE),
-        in_specs=[spec()] * 4,
-        out_specs=spec(),
+        whole_kernel,
+        out_shape=jax.ShapeDtypeStruct((4, CORE, CORE), F32),
+        in_specs=[pl.BlockSpec(memory_space=pltpu.SMEM), vmem, vmem] + [anywhere] * 4,
+        out_specs=vmem,
         scratch_shapes=[
+            pltpu.VMEM((2, PROBE, PROBE), F32),
+            pltpu.VMEM((PROBE, PROBE), F32),
+            pltpu.VMEM((PROBE, PROBE), F32),
+            pltpu.VMEM(tab.shape, BF16),
+            pltpu.VMEM((4, ROWS, COLS), F32),
+            pltpu.VMEM((CORE + 16, COLS), F32),
+            pltpu.VMEM((4, ROWS, PROBE), F32),
             pltpu.VMEM((4, ROWS, CORE), F32),
             pltpu.VMEM((4, ROWS, CORE), F32),
-            pltpu.VMEM((5, ROWS, CORE), F32),
-            pltpu.VMEM((5, BAND, CORE), F32),
-            pltpu.VMEM((5, UPROWS, CORE), F32),
-            pltpu.SemaphoreType.DMA((18,)),
-            pltpu.SemaphoreType.DMA((18,)),
+            pltpu.VMEM((4, ROWS, CORE), F32),
+            pltpu.VMEM((4, ROWS, CORE), F32),
+            pltpu.VMEM((2, 32, CORE), F32),
+            pltpu.VMEM((4, BAND, CORE), F32),
+            pltpu.VMEM((4, UPROWS, CORE), F32),
+            pltpu.VMEM((32, CORE), F32),
+            pltpu.VMEM((32, CORE), F32),
+            pltpu.SemaphoreType.DMA((58,)),
+            pltpu.SemaphoreType.DMA((58,)),
+            pltpu.SemaphoreType.DMA((4,)),
         ],
-        compiler_params=pltpu.CompilerParams(collective_id=1, has_side_effects=True),
-        name="fold",
-    )(own, lband, ext, wext)
+        compiler_params=pltpu.CompilerParams(collective_id=0, has_side_effects=True),
+        name="ptycho",
+    )(
+        positions.reshape(2), transmission.reshape(4, CORE, CORE), tv_weight, probe, fresnel_phase,
+        amplitudes.reshape(PROBE, PROBE), jnp.asarray(tab),
+    )
     return out.reshape(2, 2, CORE, CORE)
 
 

time: 57.5 us -> 43.5 us (0.76)
  Pallas kernels: 55.6 us -> 41.2 us
    pallas_call x3 -> x1, Pallas kernels: 55.6 us -> 41.2 us  [body(): pl.pallas_call(whole_kernel, out_shape=jax.ShapeDtypeStruct((4, CORE, COR...]
where the time goes in v2:
time: 43.5 us; the launch traced here: 42.9 us
  Pallas kernels  41.2 us (95%)
  local copies, waits for them, and re-layouts  1.67 us (4%)
    pallas_call x1, Pallas kernels, body(): pl.pallas_call(whole_kernel, out_shape=jax.ShapeDtypeStruct((4, CORE, COR...  41.2 us
    unnamed x1, local copies, waits for them, and re-layouts  1.67 us

profile of v2, /device:TPU:9, one launch (start us, length us, event | category | flops | bytes accessed | tf_op | source)
XLA Modules:
  0.0 42.9 jit_solution(12702513729109584769)
XLA Ops:
  0.0 41.2 %ptycho.1 = f32[4,128,128]{2,1,0:T(8,128)} custom-call(s32[2]{0:T(128)} %bitcast.7, f32[4,128,128]{2,1,0:T(8,128)} %bitcast.5, f32[128,128]{1,0:T(8,128)} %w.1, f32[2,256,256]{2,1,0:T(8,128)} %probe_any.1, f32[256,256]{1,0:T(8,128)} %phase_any.1, f32[256,256]{1,0:T(8,128)} %bitcast.6, bf16[10,256,256]{2,1,0:T(8,128)(2,1)} %constant.2.clone.tab_any), custom_call_target="tpu_custom_call" | custom-call | tf_op jit(solution)/shard_map/ptycho/pallas_call | solution.py:362
  41.2 1.7 %copy.9 = f32[2,2,128,128]{3,2,1,0:T(8,128)} copy(f32[2,2,128,128]{3,2,1,0:T(8,128)} %bitcast.4) | data formatting | bytes 524288

commit v3 on v2

--- a/solution.py
+++ b/solution.py
@@ -113,9 +113,14 @@
         self.r, self.c = lax.axis_index("row"), lax.axis_index("col")
         nr, nc = lax.axis_size("row"), lax.axis_size("col")
         self.has = {"up": self.r > 0, "down": self.r < nr - 1, "left": self.c > 0, "right": self.c < nc - 1}
+        self.relay = nr % 2 == 0
+        self.has["up2"], self.has["down2"] = self.r > 1, self.r < nr - 2
+        odd = lax.rem(self.r, 2) == 1
+        self.odd, self.even = odd, jnp.logical_not(odd)
         self.to = {"up": {"row": self.r - 1}, "down": {"row": self.r + 1}, "left": {"col": self.c - 1}, "right": {"col": self.c + 1}}
 
     def barrier(self):
+        self.to["up2"], self.to["down2"] = {"row": self.r - 2}, {"row": self.r + 2}
         sem = pltpu.get_barrier_semaphore()
         for side in OPPOSITE:
             @pl.when(self.has[side])
@@ -124,18 +129,18 @@
         pl.semaphore_wait(sem, sum(self.has[side].astype(jnp.int32) for side in OPPOSITE))
 
 
-OPPOSITE = {"up": "down", "down": "up", "left": "right", "right": "left"}
+OPPOSITE = {"up": "down", "down": "up", "left": "right", "right": "left", "up2": "down2", "down2": "up2"}
 
 
 class Copy:
-    def __init__(self, place, side, src, dst, sems, i, also=None):
+    def __init__(self, place, side, src, dst, sems, i, also=None, gets=None):
         self.op = pltpu.make_async_remote_copy(
             src_ref=src, dst_ref=dst, send_sem=sems[0].at[i], recv_sem=sems[1].at[i],
             device_id=place.to[side], device_id_type=MESH,
         )
         self.sends, self.gets = place.has[side], place.has[OPPOSITE[side]]
         if also is not None:
-            self.sends, self.gets = self.sends & also, self.gets & also
+            self.sends, self.gets = self.sends & also, self.gets & (also if gets is None else gets)
 
     def start(self):
         pl.when(self.sends)(lambda: self.op.start())
@@ -148,7 +153,7 @@
 
 
 def whole_kernel(
-    pos, tr, w, probe_any, phase_any, amp_any, tab_any, out,
+    pos, tr, w, probe_any, phase_any, amp_any, tab_any, out, last,
     probe, phase_ref, amp, tab, ext, wext, own, lband, from_left, from_right,
     total, pack, from_up, from_down, pack_up, pack_down, send, recv, local,
 ):
@@ -164,29 +169,56 @@
     mid = pl.ds(CORE, CORE)
     lanes = {"left": pl.ds(2 * CORE, CORE), "right": pl.ds(0, CORE)}
     jobs = [(BAND, tr.at[ch], ext.at[ch]) for ch in range(4)] + [(8, w, wext)]
-    copies, corners = [], []
+    copies, corners, parts, relays = [], [], [], []
+    odd, even = place.odd, place.even
+    odd_to_even, even_to_odd = ((odd, even), (even, odd)) if place.relay else ((), ())
+    own_rows = CORE - BAND
+    common = BAND - own_rows
     for ch, (band, src, dst) in enumerate(jobs):
         base = 8 * ch
         top, low = pl.ds(0, band), pl.ds(band + CORE, band)
         group = [
-            Copy(place, "up", src.at[pl.ds(0, band)], dst.at[low, mid], sems, base),
-            Copy(place, "down", src.at[pl.ds(CORE - band, band)], dst.at[top, mid], sems, base + 1),
+            Copy(place, "up", src.at[pl.ds(0, band)], dst.at[low, mid], sems, base, *(odd_to_even if ch < 4 else ())),
+            Copy(place, "down", src.at[pl.ds(CORE - band, band)], dst.at[top, mid], sems, base + 1, *(even_to_odd if ch < 4 else ())),
             Copy(place, "left", src, dst.at[pl.ds(band, CORE), lanes["left"]], sems, base + 2),
             Copy(place, "right", src, dst.at[pl.ds(band, CORE), lanes["right"]], sems, base + 3),
         ]
         for c in group:
             c.start()
         copies.append(group)
+        if ch < 4 and place.relay:
+            part = [
+                Copy(place, "up", src.at[pl.ds(0, own_rows)], dst.at[pl.ds(BAND + CORE, own_rows), mid], sems, 60 + 4 * ch, even, odd),
+                Copy(place, "down", src.at[pl.ds(BAND, own_rows)], dst.at[pl.ds(common, own_rows), mid], sems, 61 + 4 * ch, odd, even),
+            ]
+            for c in part:
+                c.start()
+            parts.append(part)
+            held_top, held_low = pl.ds(0, common), pl.ds(BAND + CORE + own_rows, common)
+            relays.append([
+                Copy(place, "up2", dst.at[held_top, mid], dst.at[held_low, mid], sems, 62 + 4 * ch, odd),
+                Copy(place, "down2", dst.at[held_low, mid], dst.at[held_top, mid], sems, 63 + 4 * ch, even),
+            ])
         corner = []
         for n, (rows, there) in enumerate(((low, has["down"]), (top, has["up"]))):
             for m, side in enumerate(("left", "right")):
                 corner.append(Copy(place, side, dst.at[rows, mid], dst.at[rows, lanes[side]], sems, base + 4 + 2 * n + m, there))
         corners.append(corner)
 
+    def forward_bands(channels):
+        for ch in channels:
+            for c in copies[ch][:2]:
+                c.got()
+            if ch < 4 and place.relay:
+                for c in relays[ch]:
+                    c.start()
+
     def forward_corners(channels):
         for ch in channels:
+            if ch < 4 and place.relay:
+                for c in parts[ch] + relays[ch]:
+                    c.got()
             for n in (0, 1):
-                copies[ch][n].got()
                 for m in (0, 1):
                     corners[ch][2 * n + m].start()
 
@@ -252,7 +284,9 @@
     kr, ki = jnp.cos(phase), jnp.sin(phase)
     measured = reorder(tab, amp[...])
     loads[3].wait()
+    forward_bands((0, 1))
     forward_corners((0, 1))
+    forward_bands((2, 3))
     arrived((0, 1))
     ar, ai = window(0), window(1)
     pr, pi = probe[0], probe[1]
@@ -260,6 +294,7 @@
     forward_corners((2, 3))
     wr, wi = inverse(tab, kr * fr - ki * fi, kr * fi + ki * fr)
     arrived((2, 3))
+    forward_bands((4,))
     forward_corners((4,))
     br, bi = window(2), window(3)
     fr, fi = forward(tab, br * wr - bi * wi, br * wi + bi * wr)
@@ -283,31 +318,39 @@
         for c in pair:
             c.start()
         along.append(pair)
-        return pltpu.roll(rest, 8 * ch, 1) if ch else rest
+        return pltpu.roll(rest, 8, 1) if ch % 2 else rest
 
     fr, fi = forward(tab, br * gr + bi * gi, br * gi - bi * gr)
     gr, gi = inverse(tab, kr * fr + ki * fi, kr * fi - ki * fr)
+    border = {2: fold(2)}
     put(0, pr * gr + pi * gi)
     put(1, pr * gi - pi * gr)
-    packed = fold(2) + fold(3) + fold(0) + fold(1)
 
     def compact(rows):
         rows = cat(rows, jnp.zeros((CORE - rows.shape[0], CORE), F32), 0)
-        parts = [rows[32 * k : 32 * k + 32] for k in range(4)]
-        return parts[0] + sum(pltpu.roll(parts[k], 32 * k, 1) for k in (1, 2, 3))
+        return rows[:16] + sum(pltpu.roll(rows[16 * k : 16 * k + 16], 16 * k, 1) for k in range(1, 8))
 
     def spread_out(x):
-        return jnp.concatenate([x] + [pltpu.roll(x, CORE - 32 * k, 1) for k in (1, 2, 3)], axis=0)
-
-    pack[0] = compact(packed[ROWS - BAND :])
-    pack[1] = compact(packed[:UPROWS])
-    pair = (
-        Copy(place, "down", pack.at[0], pack_up, sems, 56),
-        Copy(place, "up", pack.at[1], pack_down, sems, 57),
-    )
-    for c in pair:
-        c.start()
-    along.append(pair)
+        return jnp.concatenate([x] + [pltpu.roll(x, CORE - 16 * k, 1) for k in range(1, 8)], axis=0)
+
+    def send_border(sl):
+        packed = border[2 * sl] + border[2 * sl + 1]
+        pack[sl, 0] = compact(packed[ROWS - BAND :])
+        pack[sl, 1] = compact(packed[:UPROWS])
+        pair = (
+            Copy(place, "down", pack.at[sl, 0], pack_up.at[sl], sems, 56 + 2 * sl),
+            Copy(place, "up", pack.at[sl, 1], pack_down.at[sl], sems, 57 + 2 * sl),
+        )
+        for c in pair:
+            c.start()
+        along.append(pair)
+        return packed
+
+    border[3] = fold(3)
+    packed = {1: send_border(1)}
+    border[0] = fold(0)
+    border[1] = fold(1)
+    packed[0] = send_border(0)
 
     arrived((4,))
     shape = (TVROWS, PROBE)
@@ -319,39 +362,40 @@
     def cut(ref_rows):
         return pltpu.roll(ref_rows, COLS - (CORE - REACH), 1)[:, :PROBE]
 
-    weight = cut(wext[8 - REACH : 8 - REACH + TVROWS, :]) * inside
-    for pair in along:
-        for c in pair:
-            c.got()
-
     def joined(mine, upper, lower):
         upper = cat(upper, jnp.zeros((TVROWS - BAND, CORE), F32), 0)
         lower = cat(jnp.zeros((TVROWS - UPROWS, CORE), F32), lower, 0)
         return mine[BAND : BAND + TVROWS] + upper + lower
 
-    side = joined(packed, spread_out(pack_up[...])[:BAND], spread_out(pack_down[...])[:UPROWS])
-    fields = []
-    for ch in range(4):
-        grad = joined(total[ch], from_up[ch], from_down[ch])
-        rest = pltpu.roll(side, CORE - 8 * ch, 1) if ch else side
-        field = cut(ext[ch, BAND - REACH : BAND - REACH + TVROWS, :])
-        fields.append((field - LEARN_RATE * cat(grad, rest, 1)) * inside)
-    for s in range(2):
-        pair = fields[2 * s : 2 * s + 2]
-        for _ in range(TV_STEPS):
+    weight = cut(wext[8 - REACH : 8 - REACH + TVROWS, :]) * inside
+    for sl, arrivals in ((1, along[:3]), (0, along[3:])):
+        for pair in arrivals:
+            for c in pair:
+                c.got()
+        side = joined(packed[sl], spread_out(pack_up[sl])[:BAND], spread_out(pack_down[sl])[:UPROWS])
+        pair = []
+        for c in range(2):
+            ch = 2 * sl + c
+            grad = joined(total[ch], from_up[ch], from_down[ch])
+            rest = pltpu.roll(side, CORE - 8, 1) if c else side
+            field = cut(ext[ch, BAND - REACH : BAND - REACH + TVROWS, :])
+            pair.append((field - LEARN_RATE * cat(grad, rest, 1)) * inside)
+        for step in range(TV_STEPS):
             down = [pltpu.roll(f, TVROWS - 1, 0) - f for f in pair]
             along_row = [pltpu.roll(f, PROBE - 1, 1) - f for f in pair]
             square = down[0] * down[0] + along_row[0] * along_row[0] + (down[1] * down[1] + along_row[1] * along_row[1])
             gain = weight / jnp.sqrt(square + TV_EPS)
             fresh = []
-            for f, d, r in zip(pair, down, along_row):
+            for c, (f, d, r) in enumerate(zip(pair, down, along_row)):
                 d, r = gain * d, gain * r
                 update = d - pltpu.roll(d, 1, 0) + (r - pltpu.roll(r, 1, 1))
-                fresh.append((f + TV_TAU * update) * inside)
+                if step < TV_STEPS - 1:
+                    fresh.append((f + TV_TAU * update) * inside)
+                else:
+                    for ref, value in ((out, f), (last, update)):
+                        ref[2 * sl + c] = pltpu.roll(value, PROBE - REACH, 1)[REACH : REACH + CORE, :CORE]
             pair = fresh
-        for c in range(2):
-            out[2 * s + c] = pltpu.roll(pair[c], PROBE - REACH, 1)[REACH : REACH + CORE, :CORE]
-    for group in copies + corners + [across[ch] for ch in range(4)] + along:
+    for group in copies + corners + parts + relays + [across[ch] for ch in range(4)] + along:
         for c in group:
             c.sent()
 
@@ -359,11 +403,11 @@
 def body(transmission, probe, fresnel_phase, amplitudes, positions, tv_weight):
     vmem, anywhere = (pl.BlockSpec(memory_space=m) for m in (pltpu.VMEM, pl.ANY))
     tab = tables()
-    out = pl.pallas_call(
+    field, update = pl.pallas_call(
         whole_kernel,
-        out_shape=jax.ShapeDtypeStruct((4, CORE, CORE), F32),
+        out_shape=(jax.ShapeDtypeStruct((4, CORE, CORE), F32),) * 2,
         in_specs=[pl.BlockSpec(memory_space=pltpu.SMEM), vmem, vmem] + [anywhere] * 4,
-        out_specs=vmem,
+        out_specs=(vmem, vmem),
         scratch_shapes=[
             pltpu.VMEM((2, PROBE, PROBE), F32),
             pltpu.VMEM((PROBE, PROBE), F32),
@@ -376,13 +420,13 @@
             pltpu.VMEM((4, ROWS, CORE), F32),
             pltpu.VMEM((4, ROWS, CORE), F32),
             pltpu.VMEM((4, ROWS, CORE), F32),
-            pltpu.VMEM((2, 32, CORE), F32),
+            pltpu.VMEM((2, 2, 16, CORE), F32),
             pltpu.VMEM((4, BAND, CORE), F32),
             pltpu.VMEM((4, UPROWS, CORE), F32),
-            pltpu.VMEM((32, CORE), F32),
-            pltpu.VMEM((32, CORE), F32),
-            pltpu.SemaphoreType.DMA((58,)),
-            pltpu.SemaphoreType.DMA((58,)),
+            pltpu.VMEM((2, 16, CORE), F32),
+            pltpu.VMEM((2, 16, CORE), F32),
+            pltpu.SemaphoreType.DMA((76,)),
+            pltpu.SemaphoreType.DMA((76,)),
             pltpu.SemaphoreType.DMA((4,)),
         ],
         compiler_params=pltpu.CompilerParams(collective_id=0, has_side_effects=True),
@@ -391,7 +435,7 @@
         positions.reshape(2), transmission.reshape(4, CORE, CORE), tv_weight, probe, fresnel_phase,
         amplitudes.reshape(PROBE, PROBE), jnp.asarray(tab),
     )
-    return out.reshape(2, 2, CORE, CORE)
+    return (field + TV_TAU * update).reshape(2, 2, CORE, CORE)
 
 
 def solution(mesh):

time: 43.5 us -> 44.3 us (1.018)
  other arithmetic: 0 us -> 1.76 us
  local copies, waits for them, and re-layouts: 1.67 us -> 0 us
  Pallas kernels: 41.2 us -> 42.1 us
    add x0 -> x1, other arithmetic: none -> 1.76 us  [body(): return (field + TV_TAU * update).reshape(2, 2, CORE, CORE)]
    unnamed x1 -> x0, local copies, waits for them, and re-layouts: 1.67 us -> none
    pallas_call x1, Pallas kernels: 41.2 us -> 42.1 us  [body(): pl.pallas_call(whole_kernel, out_shape=(jax.ShapeDtypeStruct((4, CORE, CO...]
where the time goes in v3:
time: 44.3 us; the launch traced here: 43.9 us
  Pallas kernels  42.1 us (95%)
  other arithmetic  1.76 us (4%)
    pallas_call x1, Pallas kernels, body(): pl.pallas_call(whole_kernel, out_shape=(jax.ShapeDtypeStruct((4, CORE, CO...  42.1 us
    add x1, other arithmetic, body(): return (field + TV_TAU * update).reshape(2, 2, CORE, CORE)  1.76 us

profile of v3, /device:TPU:9, one launch (start us, length us, event | category | flops | bytes accessed | tf_op | source)
XLA Modules:
  0.0 43.9 jit_solution(12395505635688521774)
XLA Ops:
  0.0 42.1 %ptycho.1 = (f32[4,128,128]{2,1,0:T(8,128)}, f32[4,128,128]{2,1,0:T(8,128)}) custom-call(s32[2]{0:T(128)} %bitcast.6, f32[4,128,128]{2,1,0:T(8,128)} %bitcast.4, f32[128,128]{1,0:T(8,128)} %w.1, f32[2,256,256]{2,1,0:T(8,128)} %probe_any.1, f32[256,256]{1,0:T(8,128)} %phase_any.1, f32[256,256]{1,0:T(8,128)} %bitcast.5, ...), custom_call_target="tpu_custom_call" | custom-call | tf_op jit(solution)/shard_map/ptycho/pallas_call | solution.py:406
  42.1 1.8 %multiply_add_fusion = f32[4,128,128]{2,1,0:T(8,128)} fusion(f32[4,128,128]{2,1,0:T(8,128)} %get-tuple-element.7, f32[4,128,128]{2,1,0:T(8,128)} %get-tuple-element.8), kind=kLoop, calls=%fused_computation | loop fusion | flops 131072 | bytes 786432 | tf_op jit(solution)/shard_map/add | solution.py:438
